TPU v7x, 32 devices: a whole 2x2x4 slice. The times are simulated.
32 devices in a mesh: shell: 4 (over x, core), sky: 8 (over z, y).
Axes of the slice: x: 2, y: 2, z: 4, core: 2. Of those that a mesh axis runs over, the one named last changes fastest.
Arguments:
- coords: int32 [3, 4, 8, 512], P(None, 'shell', 'sky'), may hold values from 0 to 2047, as said below
- weights: bfloat16 [4, 8, 512], P('shell', 'sky'), may hold values from 0.5 to 2
- live: int32 [4, 8], P('shell', 'sky'), may hold values from 128 to 512, as said below
Outputs:
- jackknife: float32 [4, 64, 600], P('shell', 'sky')
Inputs may be any that keep to these rules, and one draw needn't show every extreme that they name: On device (a, b), coords[0] lies in [a * 256, (a+1) * 256), coords[1] in [b * 256, (b+1) * 256), coords[2] in [0, 1024). `live`: live slots are the first ones of a device; some device is full in every draw.
All inputs are finite; a program needn't handle non-finite values.
Results may differ from a plain program's by a relative error of at most 0.0003.
Values sent between devices are 32-bit elements; how exact they have to be, the bound alone decides.
A program may use at most 64 MiB of HBM per device.

v0:
```python
import math

import jax
import jax.numpy as jnp
from jax import lax
from jax.experimental import pallas as pl
from jax.experimental.pallas import tpu as pltpu
from jax.sharding import PartitionSpec as P

PART_DEV = 512
SIDE_CELLS = 256
SPAN_CELLS = 1024
SUBREGIONS = 8
S_BINS = 30
MU_BINS = 20
LANES = 128
ROWS = 8
UNROLL = 8
BIG = 1.0e6
NT = (((1,), (1,)), ((), ()))


def edge_values():
    return [int(4.0 * 10.0 ** (4.0 * level / S_BINS) + 0.5) for level in range(S_BINS + 1)]


REACH = math.isqrt(edge_values()[S_BINS] - 1)


def bin_scale(patches):
    edges = edge_values()
    factor = SIDE_CELLS * SIDE_CELLS * SPAN_CELLS / (patches * PART_DEV * PART_DEV)
    values = []
    for level in range(S_BINS):
        volume = 4.0 * math.pi / 3.0 * (edges[level + 1] ** 1.5 - edges[level] ** 1.5) / MU_BINS
        values = values + [factor / volume] * MU_BINS
    return jnp.asarray(values, dtype=jnp.float32)


def shifted(block, axis):
    count = lax.axis_size(axis)
    forward = [(i, i + 1) for i in range(count - 1)]
    backward = [(target, source) for source, target in forward]
    return lax.ppermute(block, axis, forward), lax.ppermute(block, axis, backward)


def iota_f(shape, dim):
    return lax.broadcasted_iota(jnp.int32, shape, dim).astype(jnp.float32)


def split_rows(x, y, z, w):
    xh, yh, zh = jnp.floor(x * (1 / 64)), jnp.floor(y * (1 / 64)), jnp.floor(z * (1 / 64))
    rows = [xh, yh, zh, w, x - 64 * xh, y - 64 * yh, z - 64 * zh, jnp.where(w > 0, 1.0, 0.0)]
    rows = rows + [jnp.zeros_like(x)] * 8
    return jnp.concatenate(rows, axis=0).astype(jnp.bfloat16)


def prep_kernel(tri_ref, far_ref, own_ref, meta_ref, cols, ocols):
    total = tri_ref.shape[1]
    parts = total // 3
    origin = (lax.axis_index("shell") * SIDE_CELLS).astype(jnp.float32)
    x, y, z, w = (tri_ref[c : c + 1, :] for c in range(4))
    keep = (w > 0) & (x >= origin - REACH) & (x <= origin + (SIDE_CELLS - 1 + REACH))
    wk = jnp.where(keep, w, 0.0)
    key = jnp.where(keep, z, float(SPAN_CELLS)) * total + iota_f((1, total), 1)
    cols[...] = jnp.broadcast_to(key, (8, total)).T

    def count_block(i, rank):
        col = cols[pl.ds(pl.multiple_of(i * LANES, LANES), LANES), 0:1]
        return rank + jnp.sum(jnp.where(col < key, 1.0, 0.0), axis=0, keepdims=True)

    rank = lax.fori_loop(0, total // LANES, count_block, jnp.zeros((1, total), jnp.float32))
    feats = split_rows(x, y, z, wk)

    def place(c, carry):
        dest = iota_f((LANES, total), 0) + (c * LANES).astype(jnp.float32)
        hot = jnp.where(dest == rank, 1.0, 0.0).astype(jnp.bfloat16)
        res = lax.dot_general(feats, hot, NT, preferred_element_type=jnp.float32)
        pos = 64.0 * res[0:3] + res[4:7]
        alive = res[7:8]
        zmin = jnp.min(jnp.where(alive > 0, pos[2:3], BIG), axis=1, keepdims=True)
        zmax = jnp.max(jnp.where(alive > 0, pos[2:3], -BIG), axis=1, keepdims=True)
        some = jnp.max(alive, axis=1, keepdims=True)
        shape = (1, LANES)
        far_ref[c] = jnp.concatenate(
            [pos, res[3:4], jnp.broadcast_to(zmin, shape), jnp.broadcast_to(zmax, shape),
             jnp.broadcast_to(some, shape), alive], axis=0)
        return carry

    lax.fori_loop(0, total // LANES, place, 0)

    mid = slice(parts, 2 * parts)
    x, y, z, w, key = x[:, mid], y[:, mid], z[:, mid], w[:, mid], key[:, mid]
    key_col = cols[parts : 2 * parts, 0:1]
    order = jnp.sum(jnp.where(key_col < key, 1.0, 0.0), axis=0, keepdims=True)
    region = jnp.floor(z * (SUBREGIONS / SPAN_CELLS))
    alive = w > 0
    pos = order
    for r in range(SUBREGIONS - 1):
        count = jnp.sum(jnp.where(alive & (region == r), 1.0, 0.0), axis=1, keepdims=True)
        gap = jnp.floor((count + (ROWS - 1)) * (1 / ROWS)) * ROWS - count
        pos = pos + jnp.where(region > r, gap, 0.0)
    pos = jnp.where(alive, pos, BIG)
    feats = split_rows(x, y, z, w)
    zs = jnp.concatenate([pos, z] + [pos] * 6, axis=0)
    ocols[...] = zs.T

    def place_own(c, carry):
        dest = iota_f((LANES, parts), 0) + (c * LANES).astype(jnp.float32)
        hot = jnp.where(dest == pos, 1.0, 0.0).astype(jnp.bfloat16)
        own_ref[pl.ds(pl.multiple_of(c * LANES, LANES), LANES), :] = lax.dot_general(
            hot, feats, NT, preferred_element_type=jnp.float32)
        return carry

    lax.fori_loop(0, own_ref.shape[0] // LANES, place_own, 0)
    tile = jnp.floor(ocols[:, 0:1] * (1 / ROWS))
    z_col = ocols[:, 1:2]
    mine = tile == iota_f((parts, LANES), 1)
    tmin = jnp.min(jnp.where(mine, z_col, BIG), axis=0, keepdims=True)
    tmax = jnp.max(jnp.where(mine, z_col, -BIG), axis=0, keepdims=True)
    meta_ref[...] = jnp.concatenate([tmin, tmax] + [tmin] * 6, axis=0)


def bins(dx, q):
    per_two = S_BINS / 4.0 * math.log10(2.0)
    cand = jnp.floor(jnp.log2(q) * per_two + (0.5 - 2.0 * per_two))
    edge = jnp.floor(jnp.exp2(cand * (1.0 / per_two) + 2.0) + 0.5)
    s = jnp.where(q < edge, cand - 1.0, cand)
    near = jnp.floor(jnp.abs(dx) * lax.rsqrt(q) * MU_BINS + 0.5)
    m = jnp.where(dx * dx * (MU_BINS * MU_BINS) < near * near * q, near - 1.0, near)
    return s, jnp.minimum(m, MU_BINS - 1.0)


def pair_kernel(far_ref, own_ref, meta_ref, hist_ref, plan_v, plan_s, sem):
    chunks = far_ref.shape[0] - 1
    height = plan_v.shape[0]
    edges = edge_values()
    tmin, tmax = meta_ref[0:1, :], meta_ref[1:2, :]
    slot = lax.broadcasted_iota(jnp.int32, (height, LANES), 0)
    plan = jnp.full((height, LANES), chunks, jnp.int32)
    count = jnp.zeros((1, LANES), jnp.int32)
    for c in range(chunks):
        info = far_ref[c]
        act = (info[4:5] <= tmax + REACH) & (info[5:6] >= tmin - REACH) & (info[6:7] > 0)
        plan = jnp.where((slot == count) & act, c, plan)
        count = count + jnp.where(act, 1, 0)
    region = jnp.clip(jnp.floor(tmin * (SUBREGIONS / SPAN_CELLS)), 0, SUBREGIONS - 1)
    used = jnp.sum(jnp.where(tmin < BIG, 1.0, 0.0), axis=1, keepdims=True)
    plan = jnp.where(slot == height - 1, count, plan)
    plan = jnp.where(slot == height - 2, region.astype(jnp.int32), plan)
    plan = jnp.where(slot == height - 3, used.astype(jnp.int32), plan)
    plan_v[...] = plan
    copy = pltpu.make_async_copy(plan_v, plan_s, sem)
    copy.start()
    hist_ref[...] = jnp.zeros_like(hist_ref)
    copy.wait()

    half = (16, LANES)
    low = iota_f(half, 0).astype(jnp.bfloat16)
    high = (iota_f(half, 0) + 16.0).astype(jnp.bfloat16)
    none = jnp.zeros(half, jnp.bfloat16)

    def add_tile(t, carry):
        own = own_ref[pl.ds(pl.multiple_of(t * ROWS, ROWS), ROWS), :]
        xi = jnp.broadcast_to(own[:, 0:1] * 64.0 + own[:, 4:5], (ROWS, LANES))
        yi = jnp.broadcast_to(own[:, 1:2] * 64.0 + own[:, 5:6], (ROWS, LANES))
        zi = jnp.broadcast_to(own[:, 2:3] * 64.0 + own[:, 6:7], (ROWS, LANES))
        wi = jnp.broadcast_to(own[:, 3:4], (ROWS, LANES))
        wis = [jnp.broadcast_to(wi[i : i + 1], half).astype(jnp.bfloat16) for i in range(ROWS)]

        def add_chunks(first, width, acc):
            lhs, rhs = [], []
            for u in range(width):
                info = far_ref[plan_s[first + u, t]]
                dx, dy, dz = xi - info[0:1], yi - info[1:2], zi - info[2:3]
                q = dx * dx + dy * dy + dz * dz
                s, m = bins(dx, q)
                s = jnp.where((q >= edges[0]) & (q < edges[S_BINS]), s, 99.0)
                wj = jnp.broadcast_to(info[3:4], half).astype(jnp.bfloat16)
                for i in range(ROWS):
                    si = jnp.broadcast_to(s[i : i + 1], half).astype(jnp.bfloat16)
                    mi = jnp.broadcast_to(m[i : i + 1], half).astype(jnp.bfloat16)
                    lhs.append(jnp.concatenate(
                        [jnp.where(si == low, wj, none), jnp.where(si == high, wj, none)], axis=0))
                    rhs.append(jnp.concatenate(
                        [jnp.where(mi == low, wis[i], none), jnp.where(mi == high, wis[i], none)],
                        axis=0))
            return acc + lax.dot_general(
                jnp.concatenate(lhs, axis=1), jnp.concatenate(rhs, axis=1), NT,
                preferred_element_type=jnp.float32)

        count_t = plan_s[height - 1, t]
        short = UNROLL // 2
        steps = (count_t + (short - 1)) // UNROLL
        acc = lax.fori_loop(0, steps, lambda p, acc: add_chunks(p * UNROLL, UNROLL, acc),
                            jnp.zeros((32, 32), jnp.float32))
        done = steps * UNROLL
        acc = lax.fori_loop(0, jnp.where(count_t > done, 1, 0),
                            lambda p, acc: add_chunks(done, short, acc), acc)
        r = plan_s[height - 2, t]
        hist_ref[r] = hist_ref[r] + acc
        return carry

    lax.fori_loop(0, plan_s[height - 3, 0], add_tile, 0)


def local(coords, weights, live):
    parts = coords.shape[3]
    slots = lax.iota(jnp.int32, parts)
    own_weight = jnp.where(slots < live[0, 0], weights[0, 0].astype(jnp.float32), 0.0)
    packed = jnp.concatenate(
        [coords.reshape(3, parts).astype(jnp.float32), own_weight.reshape(1, parts)], axis=0
    )
    down, up = shifted(packed, "shell")
    tri = jnp.concatenate([down, packed, up], axis=1)
    total = 3 * parts
    chunks = total // LANES
    own_rows = -(-(parts + SUBREGIONS * (ROWS - 1)) // LANES) * LANES
    vmem = pl.BlockSpec(memory_space=pltpu.VMEM)
    far, own, meta = pl.pallas_call(
        prep_kernel,
        out_shape=(
            jax.ShapeDtypeStruct((chunks, 8, LANES), jnp.float32),
            jax.ShapeDtypeStruct((own_rows, 16), jnp.float32),
            jax.ShapeDtypeStruct((8, LANES), jnp.float32),
        ),
        in_specs=[vmem],
        out_specs=(vmem, vmem, vmem),
        scratch_shapes=[pltpu.VMEM((total, 8), jnp.float32), pltpu.VMEM((parts, 8), jnp.float32)],
    )(tri)
    left, right = shifted(far, "sky")
    every = jnp.concatenate(
        [left, far, right, jnp.zeros((1, 8, LANES), jnp.float32)], axis=0
    )
    height = -(-(3 * chunks + UNROLL + 3) // 8) * 8
    hist = pl.pallas_call(
        pair_kernel,
        out_shape=jax.ShapeDtypeStruct((SUBREGIONS, 32, 32), jnp.float32),
        in_specs=[vmem, vmem, vmem],
        out_specs=vmem,
        scratch_shapes=[
            pltpu.VMEM((height, LANES), jnp.int32),
            pltpu.SMEM((height, LANES), jnp.int32),
            pltpu.SemaphoreType.DMA,
        ],
    )(every, own, meta)
    by_region = hist[:, :S_BINS, :MU_BINS].reshape(SUBREGIONS, S_BINS * MU_BINS)
    sums = lax.all_gather(jnp.sum(by_region, axis=0), "sky")
    shell_total = jnp.sum(sums, axis=0)
    scale = bin_scale(lax.axis_size("sky"))
    leave = (shell_total[None, :] - by_region) * scale[None, :]
    return leave.reshape(1, SUBREGIONS, S_BINS * MU_BINS)


def solution(mesh):
    in_specs = (P(None, "shell", "sky", None), P("shell", "sky", None), P("shell", "sky"))
    out_specs = P("shell", "sky", None)
    return jax.shard_map(local, mesh=mesh, in_specs=in_specs, out_specs=out_specs, check_vma=False)
```

profile of v0, /device:TPU:2, one launch (start us, length us, event | category | flops | bytes accessed | tf_op | source)
XLA Modules:
  0.0 97.1 jit_solution(14247456425367021128)
XLA Ops:
  0.7 0.0 copy-start.1
  0.7 0.7 fusion
  1.4 0.0 copy-done.1
  1.4 1.9 %collective-permute-start.1 = (f32[4,512]{1,0:T(4,128)S(1)}, f32[4,512]{1,0:T(4,128)S(1)}, u32[]{:S(2)}, u32[]{:S(2)}) collective-permute-start(f32[4,512]{1,0:T(4,128)S(1)} %pad_maximum_fusion.1), channel_id=1, source_target_pairs={{8,0},{16,8},{24,16},{9,1},{17,9},{25,17},{10,2},{18,10},{26,18},{... | collective-permute-start | bytes 24584 | tf_op jit(solution)/shard_map/ppermute | solution.py:44
  3.3 2.4 %collective-permute-start = (f32[4,512]{1,0:T(4,128)S(1)}, f32[4,512]{1,0:T(4,128)S(1)}, u32[]{:S(2)}, u32[]{:S(2)}) collective-permute-start(f32[4,512]{1,0:T(4,128)S(1)} %pad_maximum_fusion.1), channel_id=1, source_target_pairs={{0,8},{8,16},{16,24},{1,9},{9,17},{17,25},{2,10},{10,18},{18,26},{... | collective-permute-start | bytes 24584 | tf_op jit(solution)/shard_map/ppermute | solution.py:44
  5.7 0.0 collective-permute-done.1
  5.7 2.5 %collective-permute-done = f32[4,512]{1,0:T(4,128)S(1)} collective-permute-done((f32[4,512]{1,0:T(4,128)S(1)}, f32[4,512]{1,0:T(4,128)S(1)}, u32[]{:S(2)}, u32[]{:S(2)}) %collective-permute-start) | collective-permute-done | bytes 8224 | tf_op jit(solution)/shard_map/ppermute | solution.py:44
  8.3 0.6 pad_maximum_fusion.tri_ref
  8.9 8.7 %shard_map.46 = (f32[12,8,128]{2,1,0:T(8,128)}, f32[640,16]{1,0:T(8,128)}, f32[8,128]{1,0:T(8,128)}) custom-call(f32[4,1536]{1,0:T(4,128)} %pad_maximum_fusion.tri_ref), custom_call_target="tpu_custom_call" | custom-call | tf_op jit(solution)/shard_map/pallas_call | solution.py:220
  17.6 1.3 %collective-permute-start.3 = (f32[12,8,128]{2,1,0:T(8,128)}, f32[12,8,128]{2,1,0:T(8,128)S(1)}, u32[]{:S(2)}, u32[]{:S(2)}) collective-permute-start(f32[12,8,128]{2,1,0:T(8,128)} %get-tuple-element.8), channel_id=1, source_target_pairs={{1,0},{2,1},{3,2},{4,3},{5,4},{6,5},{7,6},{9,8},{10,9},{11,10},{12... | collective-permute-start | bytes 147464 | tf_op jit(solution)/shard_map/ppermute | solution.py:44
  18.9 4.5 %collective-permute-start.2 = (f32[12,8,128]{2,1,0:T(8,128)}, f32[12,8,128]{2,1,0:T(8,128)S(1)}, u32[]{:S(2)}, u32[]{:S(2)}) collective-permute-start(f32[12,8,128]{2,1,0:T(8,128)} %get-tuple-element.8), channel_id=1, source_target_pairs={{0,1},{1,2},{2,3},{3,4},{4,5},{5,6},{6,7},{8,9},{9,10},{10,11},{11... | collective-permute-start | bytes 147464 | tf_op jit(solution)/shard_map/ppermute | solution.py:44
  23.5 0.1 pad.3.clone
  23.5 0.3 collective-permute-done.3
  23.8 1.7 %collective-permute-done.2 = f32[12,8,128]{2,1,0:T(8,128)S(1)} collective-permute-done((f32[12,8,128]{2,1,0:T(8,128)}, f32[12,8,128]{2,1,0:T(8,128)S(1)}, u32[]{:S(2)}, u32[]{:S(2)}) %collective-permute-start.2) | collective-permute-done | bytes 49184 | tf_op jit(solution)/shard_map/ppermute | solution.py:44
  25.5 1.6 %maximum_maximum_fusion.far_ref = f32[37,8,128]{2,1,0:T(8,128)} fusion(f32[12,8,128]{2,1,0:T(8,128)S(1)} %collective-permute-done.3, f32[12,8,128]{2,1,0:T(8,128)} %get-tuple-element.8, f32[12,8,128]{2,1,0:T(8,128)S(1)} %collective-permute-done.2, f32[37]{0:T(128)S(1)} %pad.3.clone), kind=kLoop, calls=%fused_computation | loop fusion | flops 113664 | bytes 299156 | tf_op jit(solution)/shard_map/concatenate | solution.py:232
  27.1 26.0 %shard_map.47 = f32[8,32,32]{2,1,0:T(8,128)} custom-call(f32[37,8,128]{2,1,0:T(8,128)} %maximum_maximum_fusion.far_ref, f32[640,16]{1,0:T(8,128)} %get-tuple-element.9.own_ref, f32[8,128]{1,0:T(8,128)} %get-tuple-element.10.meta_ref), custom_call_target="tpu_custom_call" | custom-call | tf_op jit(solution)/shard_map/pallas_call | solution.py:236
  53.1 0.9 slice_reduce_fusion
  54.0 0.1 reshape.90
  54.2 41.7 %all-gather = f32[8,1,600]{2,1,0:T(1,128)S(1)} all-gather(f32[1,1,600]{2,1,0:T(1,128)S(1)} %reshape.90), channel_id=1, replica_groups=mesh['shell'=4,'sky'=8] {'sky'}, dimensions={0}, use_global_device_ids=true | all-gather | bytes 21600 | tf_op jit(solution)/shard_map/all_gather | solution.py:248
  95.8 0.0 copy-start
  95.8 0.1 reshape.88
  96.0 0.6 copy-done
  96.5 0.6 subtract_multiply_fusion
  (3 shorter events, 0.0 us)
Async XLA Ops:
  0.7 0.7 copy-start.1
  1.4 4.3 %collective-permute-start.1 = (f32[4,512]{1,0:T(4,128)S(1)}, f32[4,512]{1,0:T(4,128)S(1)}, u32[]{:S(2)}, u32[]{:S(2)}) collective-permute-start(f32[4,512]{1,0:T(4,128)S(1)} %pad_maximum_fusion.1), channel_id=1, source_target_pairs={{8,0},{16,8},{24,16},{9,1},{17,9},{25,17},{10,2},{18,10},{26,18},{... | collective-permute-start | bytes 24584 | tf_op jit(solution)/shard_map/ppermute | solution.py:44
  3.3 5.0 %collective-permute-start = (f32[4,512]{1,0:T(4,128)S(1)}, f32[4,512]{1,0:T(4,128)S(1)}, u32[]{:S(2)}, u32[]{:S(2)}) collective-permute-start(f32[4,512]{1,0:T(4,128)S(1)} %pad_maximum_fusion.1), channel_id=1, source_target_pairs={{0,8},{8,16},{16,24},{1,9},{9,17},{17,25},{2,10},{10,18},{18,26},{... | collective-permute-start | bytes 24584 | tf_op jit(solution)/shard_map/ppermute | solution.py:44
  17.6 6.2 %collective-permute-start.3 = (f32[12,8,128]{2,1,0:T(8,128)}, f32[12,8,128]{2,1,0:T(8,128)S(1)}, u32[]{:S(2)}, u32[]{:S(2)}) collective-permute-start(f32[12,8,128]{2,1,0:T(8,128)} %get-tuple-element.8), channel_id=1, source_target_pairs={{1,0},{2,1},{3,2},{4,3},{5,4},{6,5},{7,6},{9,8},{10,9},{11,10},{12... | collective-permute-start | bytes 147464 | tf_op jit(solution)/shard_map/ppermute | solution.py:44
  18.9 6.6 %collective-permute-start.2 = (f32[12,8,128]{2,1,0:T(8,128)}, f32[12,8,128]{2,1,0:T(8,128)S(1)}, u32[]{:S(2)}, u32[]{:S(2)}) collective-permute-start(f32[12,8,128]{2,1,0:T(8,128)} %get-tuple-element.8), channel_id=1, source_target_pairs={{0,1},{1,2},{2,3},{3,4},{4,5},{5,6},{6,7},{8,9},{9,10},{10,11},{11... | collective-permute-start | bytes 147464 | tf_op jit(solution)/shard_map/ppermute | solution.py:44
  95.8 0.7 copy-start
where the time goes:
time: 99 us; the launch traced here: 97.1 us
  blocking collectives  41.7 us (42%)
  Pallas kernels  34.8 us (35%)
  starting transfers between devices  10.2 us (10%)
  waiting for transfers between devices  4.52 us (5%)
  other arithmetic  4.46 us (5%)
    all_gather x1, blocking collectives, local(): sums = lax.all_gather(jnp.sum(by_region, axis=0), 'sky')  41.7 us
    pallas_call x1, Pallas kernels, local(): pl.pallas_call(pair_kernel, out_shape=jax.ShapeDtypeStruct((SUBREGIONS, 3...  26 us
    pallas_call x1, Pallas kernels, local(): pl.pallas_call(prep_kernel, out_shape=(jax.ShapeDtypeStruct((chunks, 8, L...  8.7 us
    ppermute x2, starting transfers between devices, shifted(): lax.ppermute(block, axis, forward)  6.95 us
    ppermute x2, waiting for transfers between devices, shifted(): lax.ppermute(block, axis, forward)  4.26 us
    ppermute x2, starting transfers between devices, shifted(): lax.ppermute(block, axis, backward)  3.2 us
  transfers between devices with their start and end apart: 4, of which 3 were waited for; matrix products, arithmetic and copies ran while one was open for 0% of the time, Pallas kernels for 0%

commit v1 on v0

--- a/solution.py
+++ b/solution.py
@@ -131,8 +131,12 @@
     return s, jnp.minimum(m, MU_BINS - 1.0)
 
 
-def pair_kernel(far_ref, own_ref, meta_ref, hist_ref, plan_v, plan_s, sem):
+def pair_kernel(left_ref, mid_ref, right_ref, own_ref, meta_ref, hist_ref, far_ref, plan_v, plan_s, sem):
     chunks = far_ref.shape[0] - 1
+    each = mid_ref.shape[0]
+    for n, ref in enumerate((left_ref, mid_ref, right_ref)):
+        far_ref[n * each : (n + 1) * each] = ref[...]
+    far_ref[chunks] = jnp.zeros((8, LANES), jnp.float32)
     height = plan_v.shape[0]
     edges = edge_values()
     tmin, tmax = meta_ref[0:1, :], meta_ref[1:2, :]
@@ -229,21 +233,19 @@
         scratch_shapes=[pltpu.VMEM((total, 8), jnp.float32), pltpu.VMEM((parts, 8), jnp.float32)],
     )(tri)
     left, right = shifted(far, "sky")
-    every = jnp.concatenate(
-        [left, far, right, jnp.zeros((1, 8, LANES), jnp.float32)], axis=0
-    )
     height = -(-(3 * chunks + UNROLL + 3) // 8) * 8
     hist = pl.pallas_call(
         pair_kernel,
         out_shape=jax.ShapeDtypeStruct((SUBREGIONS, 32, 32), jnp.float32),
-        in_specs=[vmem, vmem, vmem],
+        in_specs=[vmem] * 5,
         out_specs=vmem,
         scratch_shapes=[
+            pltpu.VMEM((3 * chunks + 1, 8, LANES), jnp.float32),
             pltpu.VMEM((height, LANES), jnp.int32),
             pltpu.SMEM((height, LANES), jnp.int32),
             pltpu.SemaphoreType.DMA,
         ],
-    )(every, own, meta)
+    )(left, far, right, own, meta)
     by_region = hist[:, :S_BINS, :MU_BINS].reshape(SUBREGIONS, S_BINS * MU_BINS)
     sums = lax.all_gather(jnp.sum(by_region, axis=0), "sky")
     shell_total = jnp.sum(sums, axis=0)

time: 99 us -> 98.5 us (level); the launches traced: 97.1 us -> 100 us
  blocking collectives: 41.7 us -> 48.4 us
  Pallas kernels: 34.8 us -> 31.9 us
  other arithmetic: 4.46 us -> 2.91 us
    all_gather x1, blocking collectives: 41.7 us -> 48.4 us  [local(): sums = lax.all_gather(jnp.sum(by_region, axis=0), 'sky')]
    pallas_call x1, Pallas kernels: 26 us -> 23.2 us  [local(): pl.pallas_call(pair_kernel, out_shape=jax.ShapeDtypeStruct((SUBREGIONS, 3...]
    concatenate x1 -> x0, other arithmetic: 1.56 us -> none  [local(): jnp.concatenate([left, far, right, jnp.zeros((1, 8, LANES), jnp.float32)]...]
where the time goes in v1:
time: 98.5 us; the launch traced here: 100 us
  blocking collectives  48.4 us (49%)
  Pallas kernels  31.9 us (32%)
  starting transfers between devices  10.2 us (10%)
  waiting for transfers between devices  4.6 us (5%)
  other arithmetic  2.91 us (3%)
  local copies, waits for them, and re-layouts  1.49 us (2%)
    all_gather x1, blocking collectives, local(): sums = lax.all_gather(jnp.sum(by_region, axis=0), 'sky')  48.4 us
    pallas_call x1, Pallas kernels, local(): pl.pallas_call(pair_kernel, out_shape=jax.ShapeDtypeStruct((SUBREGIONS, 3...  23.2 us
    pallas_call x1, Pallas kernels, local(): pl.pallas_call(prep_kernel, out_shape=(jax.ShapeDtypeStruct((chunks, 8, L...  8.7 us
    ppermute x2, starting transfers between devices, shifted(): lax.ppermute(block, axis, forward)  6.95 us
    ppermute x2, waiting for transfers between devices, shifted(): lax.ppermute(block, axis, forward)  4.26 us
    ppermute x2, starting transfers between devices, shifted(): lax.ppermute(block, axis, backward)  3.2 us
  transfers between devices with their start and end apart: 4, of which 3 were waited for; matrix products, arithmetic and copies ran while one was open for 0% of the time, Pallas kernels for 0%

profile of v1, /device:TPU:2, one launch (start us, length us, event | category | flops | bytes accessed | tf_op | source)
XLA Modules:
  0.0 100.2 jit_solution(16889498269562863910)
XLA Ops:
  0.7 0.0 copy-start.3
  0.7 0.7 fusion
  1.4 0.0 copy-done.3
  1.4 1.9 %collective-permute-start.1 = (f32[4,512]{1,0:T(4,128)S(1)}, f32[4,512]{1,0:T(4,128)S(1)}, u32[]{:S(2)}, u32[]{:S(2)}) collective-permute-start(f32[4,512]{1,0:T(4,128)S(1)} %pad_maximum_fusion.1), channel_id=1, source_target_pairs={{8,0},{16,8},{24,16},{9,1},{17,9},{25,17},{10,2},{18,10},{26,18},{... | collective-permute-start | bytes 24584 | tf_op jit(solution)/shard_map/ppermute | solution.py:44
  3.3 2.4 %collective-permute-start = (f32[4,512]{1,0:T(4,128)S(1)}, f32[4,512]{1,0:T(4,128)S(1)}, u32[]{:S(2)}, u32[]{:S(2)}) collective-permute-start(f32[4,512]{1,0:T(4,128)S(1)} %pad_maximum_fusion.1), channel_id=1, source_target_pairs={{0,8},{8,16},{16,24},{1,9},{9,17},{17,25},{2,10},{10,18},{18,26},{... | collective-permute-start | bytes 24584 | tf_op jit(solution)/shard_map/ppermute | solution.py:44
  5.7 0.0 collective-permute-done.1
  5.7 2.5 %collective-permute-done = f32[4,512]{1,0:T(4,128)S(1)} collective-permute-done((f32[4,512]{1,0:T(4,128)S(1)}, f32[4,512]{1,0:T(4,128)S(1)}, u32[]{:S(2)}, u32[]{:S(2)}) %collective-permute-start) | collective-permute-done | bytes 8224 | tf_op jit(solution)/shard_map/ppermute | solution.py:44
  8.3 0.6 pad_maximum_fusion.tri_ref
  8.9 8.7 %shard_map.46 = (f32[12,8,128]{2,1,0:T(8,128)}, f32[640,16]{1,0:T(8,128)}, f32[8,128]{1,0:T(8,128)}) custom-call(f32[4,1536]{1,0:T(4,128)} %pad_maximum_fusion.tri_ref), custom_call_target="tpu_custom_call" | custom-call | tf_op jit(solution)/shard_map/pallas_call | solution.py:224
  17.6 1.3 %collective-permute-start.3 = (f32[12,8,128]{2,1,0:T(8,128)}, f32[12,8,128]{2,1,0:T(8,128)S(1)}, u32[]{:S(2)}, u32[]{:S(2)}) collective-permute-start(f32[12,8,128]{2,1,0:T(8,128)} %get-tuple-element.8.mid_ref), channel_id=1, source_target_pairs={{1,0},{2,1},{3,2},{4,3},{5,4},{6,5},{7,6},{9,8},{10,9},{11,10},{12... | collective-permute-start | bytes 147464 | tf_op jit(solution)/shard_map/ppermute | solution.py:44
  18.9 4.5 %collective-permute-start.2 = (f32[12,8,128]{2,1,0:T(8,128)}, f32[12,8,128]{2,1,0:T(8,128)S(1)}, u32[]{:S(2)}, u32[]{:S(2)}) collective-permute-start(f32[12,8,128]{2,1,0:T(8,128)} %get-tuple-element.8.mid_ref), channel_id=1, source_target_pairs={{0,1},{1,2},{2,3},{3,4},{4,5},{5,6},{6,7},{8,9},{9,10},{10,11},{11... | collective-permute-start | bytes 147464 | tf_op jit(solution)/shard_map/ppermute | solution.py:44
  23.5 0.3 collective-permute-done.3.right_ref
  23.8 0.0 copy-start
  23.8 1.7 %collective-permute-done.2.left_ref = f32[12,8,128]{2,1,0:T(8,128)S(1)} collective-permute-done((f32[12,8,128]{2,1,0:T(8,128)}, f32[12,8,128]{2,1,0:T(8,128)S(1)}, u32[]{:S(2)}, u32[]{:S(2)}) %collective-permute-start.2) | collective-permute-done | bytes 49184 | tf_op jit(solution)/shard_map/ppermute | solution.py:44
  25.5 0.0 copy-start.1
  25.5 0.0 copy-done
  25.5 0.6 copy-done.1
  26.1 23.2 %shard_map.47 = f32[8,32,32]{2,1,0:T(8,128)} custom-call(f32[12,8,128]{2,1,0:T(8,128)} %copy-done.1, f32[12,8,128]{2,1,0:T(8,128)} %get-tuple-element.8.mid_ref, f32[12,8,128]{2,1,0:T(8,128)} %copy-done, f32[640,16]{1,0:T(8,128)} %get-tuple-element.9.own_ref, f32[8,128]{1,0:T(8,128)} %get-tuple-element.10.meta_ref), custom_call_target="tpu_custom_call" | custom-call | tf_op jit(solution)/shard_map/pallas_call | solution.py:237
  49.3 0.9 slice_reduce_fusion
  50.3 0.1 reshape.90
  50.4 48.4 %all-gather = f32[8,1,600]{2,1,0:T(1,128)S(1)} all-gather(f32[1,1,600]{2,1,0:T(1,128)S(1)} %reshape.90), channel_id=1, replica_groups=mesh['shell'=4,'sky'=8] {'sky'}, dimensions={0}, use_global_device_ids=true | all-gather | bytes 21600 | tf_op jit(solution)/shard_map/all_gather | solution.py:250
  98.8 0.1 reshape.88
  98.9 0.0 copy-start.2
  98.9 0.6 copy-done.2
  99.6 0.6 subtract_multiply_fusion
  (3 shorter events, 0.0 us)
Async XLA Ops:
  0.7 0.7 copy-start.3
  1.4 4.3 %collective-permute-start.1 = (f32[4,512]{1,0:T(4,128)S(1)}, f32[4,512]{1,0:T(4,128)S(1)}, u32[]{:S(2)}, u32[]{:S(2)}) collective-permute-start(f32[4,512]{1,0:T(4,128)S(1)} %pad_maximum_fusion.1), channel_id=1, source_target_pairs={{8,0},{16,8},{24,16},{9,1},{17,9},{25,17},{10,2},{18,10},{26,18},{... | collective-permute-start | bytes 24584 | tf_op jit(solution)/shard_map/ppermute | solution.py:44
  3.3 5.0 %collective-permute-start = (f32[4,512]{1,0:T(4,128)S(1)}, f32[4,512]{1,0:T(4,128)S(1)}, u32[]{:S(2)}, u32[]{:S(2)}) collective-permute-start(f32[4,512]{1,0:T(4,128)S(1)} %pad_maximum_fusion.1), channel_id=1, source_target_pairs={{0,8},{8,16},{16,24},{1,9},{9,17},{17,25},{2,10},{10,18},{18,26},{... | collective-permute-start | bytes 24584 | tf_op jit(solution)/shard_map/ppermute | solution.py:44
  17.6 6.2 %collective-permute-start.3 = (f32[12,8,128]{2,1,0:T(8,128)}, f32[12,8,128]{2,1,0:T(8,128)S(1)}, u32[]{:S(2)}, u32[]{:S(2)}) collective-permute-start(f32[12,8,128]{2,1,0:T(8,128)} %get-tuple-element.8.mid_ref), channel_id=1, source_target_pairs={{1,0},{2,1},{3,2},{4,3},{5,4},{6,5},{7,6},{9,8},{10,9},{11,10},{12... | collective-permute-start | bytes 147464 | tf_op jit(solution)/shard_map/ppermute | solution.py:44
  18.9 6.6 %collective-permute-start.2 = (f32[12,8,128]{2,1,0:T(8,128)}, f32[12,8,128]{2,1,0:T(8,128)S(1)}, u32[]{:S(2)}, u32[]{:S(2)}) collective-permute-start(f32[12,8,128]{2,1,0:T(8,128)} %get-tuple-element.8.mid_ref), channel_id=1, source_target_pairs={{0,1},{1,2},{2,3},{3,4},{4,5},{5,6},{6,7},{8,9},{9,10},{10,11},{11... | collective-permute-start | bytes 147464 | tf_op jit(solution)/shard_map/ppermute | solution.py:44
  23.8 1.7 %copy-start = (f32[12,8,128]{2,1,0:T(8,128)}, f32[12,8,128]{2,1,0:T(8,128)S(1)}, u32[]{:S(2)}) copy-start(f32[12,8,128]{2,1,0:T(8,128)S(1)} %collective-permute-done.3.right_ref) | copy-start | bytes 147460
  25.5 0.6 copy-start.1
  98.9 0.7 copy-start.2
